TPU v7x, 256 devices: a whole 4x4x8 slice. The times are simulated.
256 devices in a mesh: depth: 4 (over x), scan: 64 (over z, y, core).
Axes of the slice: x: 4, y: 4, z: 8, core: 2. Of those that a mesh axis runs over, the one named last changes fastest.
Arguments:
- transmission: float32 [4, 2, 8192, 1024], P('depth', None, 'scan'), may hold values from 0.4 to 1
- probe_wave: float32 [2, 256, 256], replicated, may hold values from -5 to 5
- prop_phase: float32 [256, 256], replicated, may hold values from -3.140625 to 3.140625
- measured: float32 [256, 256, 256], P('scan'), may hold values from 0.2 to 2
- scan_rows: int32 [256], P('scan'), may hold values from 0 to 127
- scan_cols: int32 [256], P('scan'), may hold values from 0 to 768
- live_counts: int32 [64], P('scan'), may hold values from 1 to 4, 160 in all
Outputs:
- object_grad: float32 [4, 2, 8192, 1024], P('depth', None, 'scan')
Inputs may be any that keep to these rules, and one draw needn't show every extreme that they name: `live_counts`: the largest count equals 4.
All inputs are finite; a program needn't handle non-finite values. No bound on the sum of `live_counts` on one device may be relied on, other than what follows from the above.
Results may differ from a plain program's by a relative error of at most 0.035.
Values may be sent and summed in bfloat16 or wider, within the bound.
A program may use at most 64 MiB of HBM per device.

v0:
```python
import functools
import math

import jax
import jax.numpy as jnp
import numpy as np
from jax import lax
from jax.experimental import pallas as pl
from jax.experimental.pallas import tpu as pltpu
from jax.sharding import PartitionSpec as P

MESH = pl.DeviceIdType.MESH
BF16 = jnp.bfloat16
F32 = jnp.float32


def dft_blocks(pixels):
    index = np.arange(pixels)
    angles = (index[:, None] * index[None, :] % pixels) * (2.0 * math.pi / pixels)
    scale = 1.0 / math.sqrt(pixels)
    re, im = np.cos(angles) * scale, -np.sin(angles) * scale
    first = np.block([[re, -im], [im, re]])
    return jnp.asarray(first, F32).astype(BF16), jnp.asarray(first.T, F32).astype(BF16)


def kernel(
    tile_hbm, probe_hbm, phase_hbm, meas_hbm, rows_s, cols_s, live_s, t1_hbm, t2_hbm,
    out_ref,
    tile32, tile16, probe32, phase, meas, t1, t2, par_out, par_in,
    lower, upper, crops_b, crops_a, patch, prop, psi, xs, us, grads, came,
    strip_low, strip_high, got_low, got_high,
    load_sem, par_sem, tile_sem_s, tile_sem_r, meas_sem,
    bx_s, bx_r, ax_s, ax_r, gb_s, gb_r, ga_s, ga_r, strip_s, strip_r,
):
    depth = lax.axis_index("depth")
    scan = lax.axis_index("scan")
    n_depth = lax.axis_size("depth")
    n_scan = lax.axis_size("scan")
    after = lax.rem(scan + 1, n_scan)
    before = lax.rem(scan + n_scan - 1, n_scan)
    half, width = patch.shape[3], patch.shape[4]
    blocks = tile32.shape[2] // width
    slots = n_depth

    def peer(offset):
        return (lax.rem(depth + offset, n_depth), scan)

    loads = [
        pltpu.make_async_copy(tile_hbm.at[0, 0], tile32.at[0], load_sem.at[0]),
        pltpu.make_async_copy(tile_hbm.at[0, 1], tile32.at[1], load_sem.at[1]),
        pltpu.make_async_copy(probe_hbm, probe32, load_sem.at[2]),
        pltpu.make_async_copy(phase_hbm, phase, load_sem.at[3]),
        pltpu.make_async_copy(t1_hbm, t1, load_sem.at[4]),
        pltpu.make_async_copy(t2_hbm, t2, load_sem.at[5]),
    ]
    for load in loads:
        load.start()

    barrier = pltpu.get_barrier_semaphore()
    for offset in range(1, n_depth):
        pl.semaphore_signal(barrier, inc=1, device_id=peer(offset), device_id_type=MESH)
    pl.semaphore_signal(barrier, inc=1, device_id=(depth, after), device_id_type=MESH)
    pl.semaphore_signal(barrier, inc=1, device_id=(depth, before), device_id_type=MESH)
    for slot in range(slots):
        par_out[slot : slot + 1, :] = jnp.full((1, width), rows_s[slot], jnp.int32)
        par_out[slots + slot : slots + slot + 1, :] = jnp.full((1, width), cols_s[slot], jnp.int32)
    par_out[2 * slots : 2 * slots + 1, :] = jnp.full((1, width), live_s[0], jnp.int32)
    pl.semaphore_wait(barrier, n_depth + 1)

    def send(src, dst, s_sem, r_sem, device):
        return pltpu.make_async_remote_copy(
            src_ref=src, dst_ref=dst, send_sem=s_sem, recv_sem=r_sem,
            device_id=device, device_id_type=MESH,
        )

    par_copy = send(par_out, par_in, par_sem.at[0], par_sem.at[1], (depth, after))
    par_copy.start()
    tile_copies = []
    for plane in range(2):
        loads[plane].wait()
        tile16[plane] = tile32[plane].astype(BF16)
        pair = [
            send(tile16.at[plane], lower.at[plane], tile_sem_s.at[0, plane],
                 tile_sem_r.at[0, plane], (depth, after)),
            send(tile16.at[plane], upper.at[plane], tile_sem_s.at[1, plane],
                 tile_sem_r.at[1, plane], (depth, before)),
        ]
        for copy in pair:
            copy.start()
        tile_copies.append(pair)
    meas_copy = send(meas_hbm.at[depth], meas, meas_sem.at[0], meas_sem.at[1], (depth, after))
    meas_copy.start()

    row_at = lax.broadcasted_iota(jnp.int32, (half, width), 0)
    lane_at = lax.broadcasted_iota(jnp.int32, (half, width), 1)

    def block_of(slot):
        first = jnp.broadcast_to(par_in[pl.ds(slots + slot, 1), :], (half, width))
        return (first >> 8) + jnp.where(lane_at < (first & (width - 1)), 1, 0)

    def from_low(slot):
        return row_at >= jnp.broadcast_to(par_in[pl.ds(slot, 1), :], (half, width))

    par_copy.wait_recv()
    b_copies = []
    for offset in range(n_depth):
        block = block_of(lax.rem(depth + offset, n_depth))
        for plane in range(2):
            piece = tile32[plane, :, :width]
            for at in range(1, blocks):
                piece = jnp.where(block == at, tile32[plane, :, at * width : (at + 1) * width], piece)
            if offset == 0:
                patch[depth, 1, plane] = piece.astype(BF16)
            else:
                crops_b[offset - 1, plane] = piece.astype(BF16)
        if offset:
            copy = send(crops_b.at[offset - 1], patch.at[depth, 1], bx_s.at[offset - 1],
                        bx_r.at[offset - 1], peer(offset))
            copy.start()
            b_copies.append(copy)

    loads[2].wait()
    loads[3].wait()
    big_row = lax.broadcasted_iota(jnp.int32, (width, width), 0)
    big_lane = lax.broadcasted_iota(jnp.int32, (width, width), 1)
    own_row = jnp.broadcast_to(par_in[pl.ds(depth, 1), :], (width, width))
    own_col = jnp.broadcast_to(par_in[pl.ds(slots + depth, 1), :], (width, width))
    down = jnp.where(((big_row - own_row) & (width - 1)) == big_lane, 1.0, 0.0).astype(BF16)
    across = jnp.where(((big_row + own_col) & (width - 1)) == big_lane, 1.0, 0.0).astype(BF16)
    for plane in range(2):
        rolled = jnp.dot(down, probe32[plane].astype(BF16), preferred_element_type=F32)
        rolled = jnp.dot(rolled.astype(BF16), across, preferred_element_type=F32)
        psi[0, plane] = rolled.astype(BF16)
    prop[0] = jnp.cos(phase[...])
    prop[1] = jnp.sin(phase[...])

    a_copies = []
    for plane in range(2):
        for copy in tile_copies[plane]:
            copy.wait_recv()
        for offset in range(n_depth):
            slot = lax.rem(depth + offset, n_depth)
            block, low = block_of(slot), from_low(slot)
            piece = jnp.zeros((half, width), F32)
            for at in range(blocks):
                span = slice(at * width, (at + 1) * width)
                merged = jnp.where(
                    low, lower[plane, :, span].astype(F32), upper[plane, :, span].astype(F32)
                )
                piece = jnp.where(block == at, merged, piece)
            if offset == 0:
                patch[depth, 0, plane] = piece.astype(BF16)
            else:
                crops_a[offset - 1, plane] = piece.astype(BF16)
                copy = send(crops_a.at[offset - 1, plane], patch.at[depth, 0, plane],
                            ax_s.at[offset - 1, plane], ax_r.at[offset - 1, plane],
                            peer(offset))
                copy.start()
                a_copies.append(copy)

    loads[4].wait()
    loads[5].wait()

    def transform(left, right):
        inner = jnp.dot(left[...], xs[...], preferred_element_type=F32)
        us[:, :width] = inner[:width].astype(BF16)
        us[:, width:] = inner[width:].astype(BF16)
        both = jnp.dot(us[...], right[...], preferred_element_type=F32)
        return both[:, :width], both[:, width:]

    def keep(re, im):
        xs[:width] = re.astype(BF16)
        xs[width:] = im.astype(BF16)

    def forward(at, carry):
        @pl.when(at != depth)
        def _():
            offset = lax.rem(depth + n_depth - at, n_depth) - 1
            send(crops_b.at[offset], patch.at[at, 1], bx_s.at[offset], bx_r.at[offset],
                 (at, scan)).wait_recv()
            for plane in range(2):
                send(crops_a.at[offset, plane], patch.at[at, 0, plane], ax_s.at[offset, plane],
                     ax_r.at[offset, plane], (at, scan)).wait_recv()

        for part in range(2):
            span = slice(part * half, (part + 1) * half)
            tr, ti = patch[at, part, 0].astype(F32), patch[at, part, 1].astype(F32)
            pr, pi = psi[at, 0, span].astype(F32), psi[at, 1, span].astype(F32)
            xs[part * half : (part + 1) * half] = (tr * pr - ti * pi).astype(BF16)
            xs[width + part * half : width + (part + 1) * half] = (tr * pi + ti * pr).astype(BF16)
        re, im = transform(t1, t2)
        keep(re * prop[0] - im * prop[1], re * prop[1] + im * prop[0])
        re, im = transform(t2, t1)
        psi[at + 1, 0] = re.astype(BF16)
        psi[at + 1, 1] = im.astype(BF16)
        return carry

    lax.fori_loop(0, n_depth, forward, 0)

    xs[:width] = psi[n_depth, 0]
    xs[width:] = psi[n_depth, 1]
    re, im = transform(t1, t2)
    meas_copy.wait_recv()
    live = jnp.where(jnp.broadcast_to(par_in[2 * slots : 2 * slots + 1, :], (width, width)) > depth, 1.0, 0.0)
    factor = live * (1.0 - meas[...] / jnp.sqrt(re * re + im * im + 1.0))
    keep(factor * re, factor * im)
    re, im = transform(t2, t1)
    keep(re, im)

    def grad_copies(at):
        offset = lax.rem(at + n_depth - depth, n_depth) - 1
        device = (at, scan)
        found = [
            send(grads.at[at, 0, plane], came.at[depth, 0, plane], ga_s.at[offset, plane],
                 ga_r.at[offset, plane], device)
            for plane in range(2)
        ]
        found.append(
            send(grads.at[at, 1], came.at[depth, 1], gb_s.at[offset], gb_r.at[offset], device)
        )
        return found

    def backward(step, carry):
        at = n_depth - 1 - step
        re, im = transform(t1, t2)
        keep(re * prop[0] + im * prop[1], im * prop[0] - re * prop[1])
        mu_re, mu_im = transform(t2, t1)
        for part in range(2):
            span = slice(part * half, (part + 1) * half)
            re, im = mu_re[span], mu_im[span]
            tr, ti = patch[at, part, 0].astype(F32), patch[at, part, 1].astype(F32)
            pr, pi = psi[at, 0, span].astype(F32), psi[at, 1, span].astype(F32)
            grads[at, part, 0] = (pr * re + pi * im).astype(BF16)
            grads[at, part, 1] = (pr * im - pi * re).astype(BF16)
            xs[part * half : (part + 1) * half] = (tr * re + ti * im).astype(BF16)
            xs[width + part * half : width + (part + 1) * half] = (tr * im - ti * re).astype(BF16)

        @pl.when(at != depth)
        def _():
            for copy in grad_copies(at):
                copy.start()

        return carry

    lax.fori_loop(0, n_depth, backward, 0)

    def arrived(offset, part, plane):
        return send(grads.at[0, part, plane], came.at[0, part, plane], ga_s.at[offset, plane],
                    ga_r.at[offset, plane], (depth, scan))

    for part in range(2):
        for plane in range(2):
            came[depth, part, plane] = grads[depth, part, plane]
    strip_copies = []
    for plane in range(2):
        for offset in range(n_depth - 1):
            arrived(offset, 0, plane).wait_recv()
        for at in range(blocks):
            low_sum = jnp.zeros((half, width), F32)
            high_sum = jnp.zeros((half, width), F32)
            for slot in range(slots):
                value = jnp.where(block_of(slot) == at, came[slot, 0, plane].astype(F32), 0.0)
                kept = jnp.where(from_low(slot), value, 0.0)
                low_sum = low_sum + kept
                high_sum = high_sum + (value - kept)
            span = slice(at * width, (at + 1) * width)
            strip_low[plane, :, span] = low_sum.astype(BF16)
            strip_high[plane, :, span] = high_sum.astype(BF16)
        pair = [
            send(strip_low.at[plane], got_low.at[plane], strip_s.at[0, plane],
                 strip_r.at[0, plane], (depth, before)),
            send(strip_high.at[plane], got_high.at[plane], strip_s.at[1, plane],
                 strip_r.at[1, plane], (depth, after)),
        ]
        for copy in pair:
            copy.start()
        strip_copies.append(pair)

    for offset in range(n_depth - 1):
        send(grads.at[0, 1], came.at[0, 1], gb_s.at[offset], gb_r.at[offset],
             (depth, scan)).wait_recv()
    for plane in range(2):
        for at in range(blocks):
            total = jnp.zeros((half, width), F32)
            for slot in range(slots):
                total = total + jnp.where(block_of(slot) == at, came[slot, 1, plane].astype(F32), 0.0)
            tile32[plane, :, at * width : (at + 1) * width] = total
    for plane in range(2):
        for copy in strip_copies[plane]:
            copy.wait_recv()
        out_ref[0, plane] = (
            tile32[plane] + got_low[plane].astype(F32) + got_high[plane].astype(F32)
        )

    par_copy.wait_send()
    meas_copy.wait_send()
    for copy in b_copies + a_copies:
        copy.wait_send()
    for pair in tile_copies + strip_copies:
        for copy in pair:
            copy.wait_send()
    for step in range(1, n_depth):
        for copy in grad_copies(lax.rem(depth + step, n_depth)):
            copy.wait_send()


def body(transmission, probe_wave, prop_phase, measured, scan_rows, scan_cols, live_counts):
    width = probe_wave.shape[-1]
    half = transmission.shape[2]
    columns = transmission.shape[3]
    n_depth = lax.axis_size("depth")
    t1, t2 = dft_blocks(width)
    dma = pltpu.SemaphoreType.DMA
    others = n_depth - 1
    scratch = [
        pltpu.VMEM((2, half, columns), F32),
        pltpu.VMEM((2, half, columns), BF16),
        pltpu.VMEM((2, width, width), F32),
        pltpu.VMEM((width, width), F32),
        pltpu.VMEM((width, width), F32),
        pltpu.VMEM((2 * width, 2 * width), BF16),
        pltpu.VMEM((2 * width, 2 * width), BF16),
        pltpu.VMEM((16, width), jnp.int32),
        pltpu.VMEM((16, width), jnp.int32),
        pltpu.VMEM((2, half, columns), BF16),
        pltpu.VMEM((2, half, columns), BF16),
        pltpu.VMEM((others, 2, half, width), BF16),
        pltpu.VMEM((others, 2, half, width), BF16),
        pltpu.VMEM((n_depth, 2, 2, half, width), BF16),
        pltpu.VMEM((2, width, width), F32),
        pltpu.VMEM((n_depth + 1, 2, width, width), BF16),
        pltpu.VMEM((2 * width, width), BF16),
        pltpu.VMEM((width, 2 * width), BF16),
        pltpu.VMEM((n_depth, 2, 2, half, width), BF16),
        pltpu.VMEM((n_depth, 2, 2, half, width), BF16),
        pltpu.VMEM((2, half, columns), BF16),
        pltpu.VMEM((2, half, columns), BF16),
        pltpu.VMEM((2, half, columns), BF16),
        pltpu.VMEM((2, half, columns), BF16),
        dma((6,)),
        dma((2,)),
        dma((2, 2)),
        dma((2, 2)),
        dma((2,)),
        dma((others,)),
        dma((others,)),
        dma((others, 2)),
        dma((others, 2)),
        dma((others,)),
        dma((others,)),
        dma((others, 2)),
        dma((others, 2)),
        dma((2, 2)),
        dma((2, 2)),
    ]
    anywhere = pl.BlockSpec(memory_space=pl.ANY)
    scalar = pl.BlockSpec(memory_space=pltpu.SMEM)
    return pl.pallas_call(
        kernel,
        out_shape=jax.ShapeDtypeStruct(transmission.shape, F32),
        in_specs=[anywhere] * 4 + [scalar] * 3 + [anywhere] * 2,
        out_specs=pl.BlockSpec(memory_space=pltpu.VMEM),
        scratch_shapes=scratch,
        compiler_params=pltpu.CompilerParams(
            collective_id=0, has_side_effects=True, vmem_limit_bytes=48 << 20
        ),
    )(transmission, probe_wave, prop_phase, measured, scan_rows, scan_cols, live_counts, t1, t2)


def solution(mesh):
    in_specs = (
        P("depth", None, "scan", None),
        P(),
        P(),
        P("scan", None, None),
        P("scan"),
        P("scan"),
        P("scan"),
    )
    out_specs = P("depth", None, "scan", None)
    return jax.shard_map(body, mesh=mesh, in_specs=in_specs, out_specs=out_specs, check_vma=False)
```

profile of v0, /device:TPU:0, one launch (start us, length us, event | category | flops | bytes accessed | tf_op | source)
XLA Modules:
  0.0 63.0 jit_solution(10933554865305878753)
XLA Ops:
  0.0 0.0 copy-start.7
  0.0 0.0 copy-start.6
  0.7 0.0 copy-done.7
  0.7 0.0 copy-done.6
  0.7 0.0 copy-start
  0.7 1.2 %copy-done = f32[1,2,128,1024]{3,2,1,0:T(8,128)S(1)} copy-done((f32[1,2,128,1024]{3,2,1,0:T(8,128)S(1)}, f32[1,2,128,1024]{3,2,1,0:T(8,128)}, u32[]{:S(2)}) %copy-start) | copy-done | bytes 1048600
  1.9 0.0 copy-start.1
  1.9 1.2 %copy-done.1 = f32[4,256,256]{2,1,0:T(8,128)S(1)} copy-done((f32[4,256,256]{2,1,0:T(8,128)S(1)}, f32[4,256,256]{2,1,0:T(8,128)}, u32[]{:S(2)}) %copy-start.1) | copy-done | bytes 1048600
  3.2 0.0 copy-start.2
  3.2 1.0 %copy-done.2 = f32[2,256,256]{2,1,0:T(8,128)S(1)} copy-done((f32[2,256,256]{2,1,0:T(8,128)S(1)}, f32[2,256,256]{2,1,0:T(8,128)}, u32[]{:S(2)}) %copy-start.2) | copy-done | bytes 524312
  4.2 0.0 copy-start.3
  4.2 1.0 %copy-done.3 = bf16[512,512]{1,0:T(8,128)(2,1)S(1)} copy-done((bf16[512,512]{1,0:T(8,128)(2,1)S(1)}, bf16[512,512]{1,0:T(8,128)(2,1)}, u32[]{:S(2)}) %copy-start.3) | copy-done | bytes 524312
  5.2 0.0 copy-start.4
  5.2 1.0 %copy-done.4 = bf16[512,512]{1,0:T(8,128)(2,1)S(1)} copy-done((bf16[512,512]{1,0:T(8,128)(2,1)S(1)}, bf16[512,512]{1,0:T(8,128)(2,1)}, u32[]{:S(2)}) %copy-start.4) | copy-done | bytes 524312
  6.3 0.0 copy-start.5
  6.3 0.9 %copy-done.5 = f32[256,256]{1,0:T(8,128)S(1)} copy-done((f32[256,256]{1,0:T(8,128)S(1)}, f32[256,256]{1,0:T(8,128)}, u32[]{:S(2)}) %copy-start.5) | copy-done | bytes 262168
  7.2 54.8 %shard_map.91 = f32[1,2,128,1024]{3,2,1,0:T(8,128)S(1)} custom-call(f32[1,2,128,1024]{3,2,1,0:T(8,128)S(1)} %copy-done, f32[2,256,256]{2,1,0:T(8,128)S(1)} %copy-done.2, f32[256,256]{1,0:T(8,128)S(1)} %copy-done.5, f32[4,256,256]{2,1,0:T(8,128)S(1)} %copy-done.1, s32[4]{0:T(128)S(1)} %copy-done.6, s32[4]{0:T(128)S(1)} %copy-done.7, s32[1]{0:T(128)S(6)} %copy.11.live_s, ...), custom_call_target="tpu_custom_call" | custom-call | tf_op jit(solution)/shard_map/pallas_call | solution.py:358
  62.0 1.0 %copy.12 = f32[1,2,128,1024]{3,2,1,0:T(8,128)} copy(f32[1,2,128,1024]{3,2,1,0:T(8,128)S(1)} %shard_map.91) | data formatting | bytes 2097152
Async XLA Ops:
  0.0 0.7 %copy-start.7 = (s32[4]{0:T(128)S(1)}, s32[4]{0:T(128)}, u32[]{:S(2)}) copy-start(s32[4]{0:T(128)} %cols_s.1) | copy-start | bytes 52
  0.0 0.7 %copy-start.6 = (s32[4]{0:T(128)S(1)}, s32[4]{0:T(128)}, u32[]{:S(2)}) copy-start(s32[4]{0:T(128)} %rows_s.1) | copy-start | bytes 52
  0.7 1.2 %copy-start = (f32[1,2,128,1024]{3,2,1,0:T(8,128)S(1)}, f32[1,2,128,1024]{3,2,1,0:T(8,128)}, u32[]{:S(2)}) copy-start(f32[1,2,128,1024]{3,2,1,0:T(8,128)} %tile_hbm.1) | copy-start | bytes 3145732
  1.9 1.2 %copy-start.1 = (f32[4,256,256]{2,1,0:T(8,128)S(1)}, f32[4,256,256]{2,1,0:T(8,128)}, u32[]{:S(2)}) copy-start(f32[4,256,256]{2,1,0:T(8,128)} %meas_hbm.1) | copy-start | bytes 3145732
  3.2 1.0 %copy-start.2 = (f32[2,256,256]{2,1,0:T(8,128)S(1)}, f32[2,256,256]{2,1,0:T(8,128)}, u32[]{:S(2)}) copy-start(f32[2,256,256]{2,1,0:T(8,128)} %probe_hbm.1) | copy-start | bytes 1572868
  4.2 1.0 %copy-start.3 = (bf16[512,512]{1,0:T(8,128)(2,1)S(1)}, bf16[512,512]{1,0:T(8,128)(2,1)}, u32[]{:S(2)}) copy-start(bf16[512,512]{1,0:T(8,128)(2,1)} %constant.12.t2_hbm) | copy-start | bytes 1572868
  5.2 1.0 %copy-start.4 = (bf16[512,512]{1,0:T(8,128)(2,1)S(1)}, bf16[512,512]{1,0:T(8,128)(2,1)}, u32[]{:S(2)}) copy-start(bf16[512,512]{1,0:T(8,128)(2,1)} %constant.11.t1_hbm) | copy-start | bytes 1572868
  6.3 0.9 %copy-start.5 = (f32[256,256]{1,0:T(8,128)S(1)}, f32[256,256]{1,0:T(8,128)}, u32[]{:S(2)}) copy-start(f32[256,256]{1,0:T(8,128)} %phase_hbm.1) | copy-start | bytes 786436
where the time goes:
time: 63.3 us; the launch traced here: 63 us
  Pallas kernels  54.8 us (87%)
  local copies, waits for them, and re-layouts  7.49 us (12%)
  between operations  0.72 us (1%)
    pallas_call x1, Pallas kernels, body(): pl.pallas_call(kernel, out_shape=jax.ShapeDtypeStruct(transmission.shape,...  54.8 us
    unnamed x17, local copies, waits for them, and re-layouts  7.49 us

commit v1 on v0

--- a/solution.py
+++ b/solution.py
@@ -24,11 +24,11 @@
 
 
 def kernel(
-    tile_hbm, probe_hbm, phase_hbm, meas_hbm, rows_s, cols_s, live_s, t1_hbm, t2_hbm,
-    out_ref,
-    tile32, tile16, probe32, phase, meas, t1, t2, par_out, par_in,
+    tile_hbm, probe_hbm, phase_hbm, meas_hbm, rows_hbm, cols_hbm, live_hbm, t1_hbm, t2_hbm,
+    own_hbm, got_low, got_high,
+    rows_s, cols_s, live_s, blk, low, tile32, tile16, probe32, phase, meas, t1, t2, par_out, par_in,
     lower, upper, crops_b, crops_a, patch, prop, psi, xs, us, grads, came,
-    strip_low, strip_high, got_low, got_high,
+    strip_low, strip_high,
     load_sem, par_sem, tile_sem_s, tile_sem_r, meas_sem,
     bx_s, bx_r, ax_s, ax_r, gb_s, gb_r, ga_s, ga_r, strip_s, strip_r,
 ):
@@ -41,6 +41,8 @@
     half, width = patch.shape[3], patch.shape[4]
     blocks = tile32.shape[2] // width
     slots = n_depth
+    rows = half // 2
+    chunks = [(plane, slice(part * rows, (part + 1) * rows)) for plane in range(2) for part in range(2)]
 
     def peer(offset):
         return (lax.rem(depth + offset, n_depth), scan)
@@ -52,6 +54,9 @@
         pltpu.make_async_copy(phase_hbm, phase, load_sem.at[3]),
         pltpu.make_async_copy(t1_hbm, t1, load_sem.at[4]),
         pltpu.make_async_copy(t2_hbm, t2, load_sem.at[5]),
+        pltpu.make_async_copy(rows_hbm, rows_s, load_sem.at[6]),
+        pltpu.make_async_copy(cols_hbm, cols_s, load_sem.at[7]),
+        pltpu.make_async_copy(live_hbm, live_s, load_sem.at[8]),
     ]
     for load in loads:
         load.start()
@@ -61,6 +66,8 @@
         pl.semaphore_signal(barrier, inc=1, device_id=peer(offset), device_id_type=MESH)
     pl.semaphore_signal(barrier, inc=1, device_id=(depth, after), device_id_type=MESH)
     pl.semaphore_signal(barrier, inc=1, device_id=(depth, before), device_id_type=MESH)
+    for load in loads[6:]:
+        load.wait()
     for slot in range(slots):
         par_out[slot : slot + 1, :] = jnp.full((1, width), rows_s[slot], jnp.int32)
         par_out[slots + slot : slots + slot + 1, :] = jnp.full((1, width), cols_s[slot], jnp.int32)
@@ -76,14 +83,15 @@
     par_copy = send(par_out, par_in, par_sem.at[0], par_sem.at[1], (depth, after))
     par_copy.start()
     tile_copies = []
-    for plane in range(2):
-        loads[plane].wait()
-        tile16[plane] = tile32[plane].astype(BF16)
+    for at, (plane, span) in enumerate(chunks):
+        if at % 2 == 0:
+            loads[plane].wait()
+        tile16[plane, span] = tile32[plane, span].astype(BF16)
         pair = [
-            send(tile16.at[plane], lower.at[plane], tile_sem_s.at[0, plane],
-                 tile_sem_r.at[0, plane], (depth, after)),
-            send(tile16.at[plane], upper.at[plane], tile_sem_s.at[1, plane],
-                 tile_sem_r.at[1, plane], (depth, before)),
+            send(tile16.at[plane, span], lower.at[plane, span], tile_sem_s.at[0, at],
+                 tile_sem_r.at[0, at], (depth, after)),
+            send(tile16.at[plane, span], upper.at[plane, span], tile_sem_s.at[1, at],
+                 tile_sem_r.at[1, at], (depth, before)),
         ]
         for copy in pair:
             copy.start()
@@ -91,28 +99,34 @@
     meas_copy = send(meas_hbm.at[depth], meas, meas_sem.at[0], meas_sem.at[1], (depth, after))
     meas_copy.start()
 
+    par_copy.wait_recv()
     row_at = lax.broadcasted_iota(jnp.int32, (half, width), 0)
-    lane_at = lax.broadcasted_iota(jnp.int32, (half, width), 1)
-
-    def block_of(slot):
-        first = jnp.broadcast_to(par_in[pl.ds(slots + slot, 1), :], (half, width))
-        return (first >> 8) + jnp.where(lane_at < (first & (width - 1)), 1, 0)
-
-    def from_low(slot):
-        return row_at >= jnp.broadcast_to(par_in[pl.ds(slot, 1), :], (half, width))
-
-    par_copy.wait_recv()
+    lane_at = lax.broadcasted_iota(jnp.int32, (rows, width), 1)
+    for slot in range(slots):
+        first = jnp.broadcast_to(par_in[slots + slot : slots + slot + 1, :], (rows, width))
+        block = (first >> 8) + jnp.where(lane_at < (first & (width - 1)), 1, 0)
+        blk[slot] = block.astype(F32).astype(BF16)
+        begin = jnp.broadcast_to(par_in[slot : slot + 1, :], (half, width))
+        low[slot] = jnp.where(row_at >= begin, 1.0, 0.0).astype(BF16)
+
+    def pick(slot, values):
+        piece = values[0]
+        for at in range(1, blocks):
+            piece = jnp.where(blk[slot] == at, values[at], piece)
+        return piece
+
+    def columns(at):
+        return slice(at * width, (at + 1) * width)
+
     b_copies = []
     for offset in range(n_depth):
-        block = block_of(lax.rem(depth + offset, n_depth))
-        for plane in range(2):
-            piece = tile32[plane, :, :width]
-            for at in range(1, blocks):
-                piece = jnp.where(block == at, tile32[plane, :, at * width : (at + 1) * width], piece)
+        slot = lax.rem(depth + offset, n_depth)
+        for plane, span in chunks:
+            piece = pick(slot, [tile16[plane, span, columns(at)] for at in range(blocks)])
             if offset == 0:
-                patch[depth, 1, plane] = piece.astype(BF16)
+                patch[depth, 1, plane, span] = piece
             else:
-                crops_b[offset - 1, plane] = piece.astype(BF16)
+                crops_b[offset - 1, plane, span] = piece
         if offset:
             copy = send(crops_b.at[offset - 1], patch.at[depth, 1], bx_s.at[offset - 1],
                         bx_r.at[offset - 1], peer(offset))
@@ -135,25 +149,22 @@
     prop[1] = jnp.sin(phase[...])
 
     a_copies = []
-    for plane in range(2):
-        for copy in tile_copies[plane]:
+    for number, (plane, span) in enumerate(chunks):
+        for copy in tile_copies[number]:
             copy.wait_recv()
-        for offset in range(n_depth):
+        for offset in (1, 3, 2, 0) if n_depth == 4 else range(n_depth):
             slot = lax.rem(depth + offset, n_depth)
-            block, low = block_of(slot), from_low(slot)
-            piece = jnp.zeros((half, width), F32)
-            for at in range(blocks):
-                span = slice(at * width, (at + 1) * width)
-                merged = jnp.where(
-                    low, lower[plane, :, span].astype(F32), upper[plane, :, span].astype(F32)
-                )
-                piece = jnp.where(block == at, merged, piece)
+            is_low = low[slot, span] > 0.5
+            piece = pick(slot, [
+                jnp.where(is_low, lower[plane, span, columns(at)], upper[plane, span, columns(at)])
+                for at in range(blocks)
+            ])
             if offset == 0:
-                patch[depth, 0, plane] = piece.astype(BF16)
+                patch[depth, 0, plane, span] = piece
             else:
-                crops_a[offset - 1, plane] = piece.astype(BF16)
-                copy = send(crops_a.at[offset - 1, plane], patch.at[depth, 0, plane],
-                            ax_s.at[offset - 1, plane], ax_r.at[offset - 1, plane],
+                crops_a[offset - 1, plane, span] = piece
+                copy = send(crops_a.at[offset - 1, plane, span], patch.at[depth, 0, plane, span],
+                            ax_s.at[offset - 1, number], ax_r.at[offset - 1, number],
                             peer(offset))
                 copy.start()
                 a_copies.append(copy)
@@ -178,9 +189,10 @@
             offset = lax.rem(depth + n_depth - at, n_depth) - 1
             send(crops_b.at[offset], patch.at[at, 1], bx_s.at[offset], bx_r.at[offset],
                  (at, scan)).wait_recv()
-            for plane in range(2):
-                send(crops_a.at[offset, plane], patch.at[at, 0, plane], ax_s.at[offset, plane],
-                     ax_r.at[offset, plane], (at, scan)).wait_recv()
+            for number, (plane, rows_at) in enumerate(chunks):
+                send(crops_a.at[offset, plane, rows_at], patch.at[at, 0, plane, rows_at],
+                     ax_s.at[offset, number], ax_r.at[offset, number],
+                     (at, scan)).wait_recv()
 
         for part in range(2):
             span = slice(part * half, (part + 1) * half)
@@ -207,18 +219,18 @@
     re, im = transform(t2, t1)
     keep(re, im)
 
-    def grad_copies(at):
+    def grad_near(at):
         offset = lax.rem(at + n_depth - depth, n_depth) - 1
-        device = (at, scan)
-        found = [
-            send(grads.at[at, 0, plane], came.at[depth, 0, plane], ga_s.at[offset, plane],
-                 ga_r.at[offset, plane], device)
-            for plane in range(2)
+        return [
+            send(grads.at[at, 0, plane, span], came.at[depth, 0, plane, span],
+                 ga_s.at[offset, number], ga_r.at[offset, number], (at, scan))
+            for number, (plane, span) in enumerate(chunks)
         ]
-        found.append(
-            send(grads.at[at, 1], came.at[depth, 1], gb_s.at[offset], gb_r.at[offset], device)
-        )
-        return found
+
+    def grad_far(at):
+        offset = lax.rem(at + n_depth - depth, n_depth) - 1
+        return send(grads.at[at, 1], came.at[depth, 1], gb_s.at[offset], gb_r.at[offset],
+                    (at, scan))
 
     def backward(step, carry):
         at = n_depth - 1 - step
@@ -237,40 +249,51 @@
 
         @pl.when(at != depth)
         def _():
-            for copy in grad_copies(at):
+            for copy in grad_near(at):
                 copy.start()
 
         return carry
 
     lax.fori_loop(0, n_depth, backward, 0)
 
-    def arrived(offset, part, plane):
-        return send(grads.at[0, part, plane], came.at[0, part, plane], ga_s.at[offset, plane],
-                    ga_r.at[offset, plane], (depth, scan))
+    for back in range(n_depth):
+        at = n_depth - 1 - back
+
+        @pl.when(at != depth)
+        def _(at=at):
+            grad_far(at).start()
 
     for part in range(2):
         for plane in range(2):
             came[depth, part, plane] = grads[depth, part, plane]
+    zero = jnp.zeros((rows // 2, width), BF16)
     strip_copies = []
-    for plane in range(2):
+    for number, (plane, span) in enumerate(chunks):
         for offset in range(n_depth - 1):
-            arrived(offset, 0, plane).wait_recv()
-        for at in range(blocks):
-            low_sum = jnp.zeros((half, width), F32)
-            high_sum = jnp.zeros((half, width), F32)
+            send(grads.at[0, 0, plane, span], came.at[0, 0, plane, span], ga_s.at[offset, number],
+                 ga_r.at[offset, number], (depth, scan)).wait_recv()
+        for piece in range(2):
+            start = span.start + piece * (rows // 2)
+            at_rows = slice(start, start + rows // 2)
+            lows, highs = [], []
             for slot in range(slots):
-                value = jnp.where(block_of(slot) == at, came[slot, 0, plane].astype(F32), 0.0)
-                kept = jnp.where(from_low(slot), value, 0.0)
-                low_sum = low_sum + kept
-                high_sum = high_sum + (value - kept)
-            span = slice(at * width, (at + 1) * width)
-            strip_low[plane, :, span] = low_sum.astype(BF16)
-            strip_high[plane, :, span] = high_sum.astype(BF16)
+                value = came[slot, 0, plane, at_rows]
+                is_low = low[slot, at_rows] > 0.5
+                lows.append(jnp.where(is_low, value, zero))
+                highs.append(jnp.where(is_low, zero, value))
+            for at in range(blocks):
+                for target, values in ((strip_low, lows), (strip_high, highs)):
+                    terms = [
+                        jnp.where(blk[slot, : rows // 2] == at, values[slot], zero)
+                        for slot in range(slots)
+                    ]
+                    total = (terms[0] + terms[1]) + (terms[2] + terms[3])
+                    target[plane, at_rows, columns(at)] = total
         pair = [
-            send(strip_low.at[plane], got_low.at[plane], strip_s.at[0, plane],
-                 strip_r.at[0, plane], (depth, before)),
-            send(strip_high.at[plane], got_high.at[plane], strip_s.at[1, plane],
-                 strip_r.at[1, plane], (depth, after)),
+            send(strip_low.at[plane, span], got_low.at[plane, span], strip_s.at[0, number],
+                 strip_r.at[0, number], (depth, before)),
+            send(strip_high.at[plane, span], got_high.at[plane, span], strip_s.at[1, number],
+                 strip_r.at[1, number], (depth, after)),
         ]
         for copy in pair:
             copy.start()
@@ -279,18 +302,26 @@
     for offset in range(n_depth - 1):
         send(grads.at[0, 1], came.at[0, 1], gb_s.at[offset], gb_r.at[offset],
              (depth, scan)).wait_recv()
+    stores = []
     for plane in range(2):
-        for at in range(blocks):
-            total = jnp.zeros((half, width), F32)
-            for slot in range(slots):
-                total = total + jnp.where(block_of(slot) == at, came[slot, 1, plane].astype(F32), 0.0)
-            tile32[plane, :, at * width : (at + 1) * width] = total
-    for plane in range(2):
-        for copy in strip_copies[plane]:
+        for piece in range(4):
+            at_rows = slice(piece * (rows // 2), (piece + 1) * (rows // 2))
+            values = [came[slot, 1, plane, at_rows] for slot in range(slots)]
+            for at in range(blocks):
+                terms = [
+                    jnp.where(blk[slot, : rows // 2] == at, values[slot], zero).astype(F32)
+                    for slot in range(slots)
+                ]
+                total = (terms[0] + terms[1]) + (terms[2] + terms[3])
+                tile32[plane, at_rows, columns(at)] = total
+        store = pltpu.make_async_copy(tile32.at[plane], own_hbm.at[plane], load_sem.at[plane])
+        store.start()
+        stores.append(store)
+    for pair in strip_copies:
+        for copy in pair:
             copy.wait_recv()
-        out_ref[0, plane] = (
-            tile32[plane] + got_low[plane].astype(F32) + got_high[plane].astype(F32)
-        )
+    for store in stores:
+        store.wait()
 
     par_copy.wait_send()
     meas_copy.wait_send()
@@ -300,7 +331,8 @@
         for copy in pair:
             copy.wait_send()
     for step in range(1, n_depth):
-        for copy in grad_copies(lax.rem(depth + step, n_depth)):
+        at = lax.rem(depth + step, n_depth)
+        for copy in grad_near(at) + [grad_far(at)]:
             copy.wait_send()
 
 
@@ -313,6 +345,11 @@
     dma = pltpu.SemaphoreType.DMA
     others = n_depth - 1
     scratch = [
+        pltpu.SMEM((n_depth,), jnp.int32),
+        pltpu.SMEM((n_depth,), jnp.int32),
+        pltpu.SMEM((1,), jnp.int32),
+        pltpu.VMEM((n_depth, half // 2, width), BF16),
+        pltpu.VMEM((n_depth, half, width), BF16),
         pltpu.VMEM((2, half, columns), F32),
         pltpu.VMEM((2, half, columns), BF16),
         pltpu.VMEM((2, width, width), F32),
@@ -335,36 +372,38 @@
         pltpu.VMEM((n_depth, 2, 2, half, width), BF16),
         pltpu.VMEM((2, half, columns), BF16),
         pltpu.VMEM((2, half, columns), BF16),
-        pltpu.VMEM((2, half, columns), BF16),
-        pltpu.VMEM((2, half, columns), BF16),
-        dma((6,)),
+        dma((9,)),
         dma((2,)),
-        dma((2, 2)),
-        dma((2, 2)),
+        dma((2, 4)),
+        dma((2, 4)),
         dma((2,)),
         dma((others,)),
         dma((others,)),
-        dma((others, 2)),
-        dma((others, 2)),
+        dma((others, 4)),
+        dma((others, 4)),
         dma((others,)),
         dma((others,)),
-        dma((others, 2)),
-        dma((others, 2)),
-        dma((2, 2)),
-        dma((2, 2)),
+        dma((others, 4)),
+        dma((others, 4)),
+        dma((2, 4)),
+        dma((2, 4)),
     ]
-    anywhere = pl.BlockSpec(memory_space=pl.ANY)
-    scalar = pl.BlockSpec(memory_space=pltpu.SMEM)
-    return pl.pallas_call(
+    anywhere = pl.BlockSpec(memory_space=pltpu.HBM)
+    own, from_after, from_before = pl.pallas_call(
         kernel,
-        out_shape=jax.ShapeDtypeStruct(transmission.shape, F32),
-        in_specs=[anywhere] * 4 + [scalar] * 3 + [anywhere] * 2,
-        out_specs=pl.BlockSpec(memory_space=pltpu.VMEM),
+        out_shape=[
+            jax.ShapeDtypeStruct((2, half, columns), F32),
+            jax.ShapeDtypeStruct((2, half, columns), BF16),
+            jax.ShapeDtypeStruct((2, half, columns), BF16),
+        ],
+        in_specs=[anywhere] * 9,
+        out_specs=[anywhere] * 3,
         scratch_shapes=scratch,
         compiler_params=pltpu.CompilerParams(
-            collective_id=0, has_side_effects=True, vmem_limit_bytes=48 << 20
+            collective_id=0, has_side_effects=True, vmem_limit_bytes=67_000_000
         ),
     )(transmission, probe_wave, prop_phase, measured, scan_rows, scan_cols, live_counts, t1, t2)
+    return (own + from_after.astype(F32) + from_before.astype(F32))[None]
 
 
 def solution(mesh):

time: 63.3 us -> 53.6 us (0.85)
  local copies, waits for them, and re-layouts: 7.49 us -> 0 us
  Pallas kernels: 54.8 us -> 50.1 us
  other arithmetic: 0 us -> 2.73 us
    unnamed x17 -> x0, local copies, waits for them, and re-layouts: 7.49 us -> none
    pallas_call x1, Pallas kernels: 54.8 us -> 50.1 us  [body(): pl.pallas_call(kernel, out_shape=[jax.ShapeDtypeStruct((2, half, columns)...]
    broadcast_in_dim x0 -> x1, other arithmetic: none -> 2.73 us  [body(): return (own + from_after.astype(F32) + from_before.astype(F32))[None]]
where the time goes in v1:
time: 53.6 us; the launch traced here: 53.5 us
  Pallas kernels  50.1 us (93%)
  other arithmetic  2.73 us (5%)
  between operations  0.66 us (1%)
    pallas_call x1, Pallas kernels, body(): pl.pallas_call(kernel, out_shape=[jax.ShapeDtypeStruct((2, half, columns)...  50.1 us
    broadcast_in_dim x1, other arithmetic, body(): return (own + from_after.astype(F32) + from_before.astype(F32))[None]  2.73 us

profile of v1, /device:TPU:0, one launch (start us, length us, event | category | flops | bytes accessed | tf_op | source)
XLA Modules:
  0.0 53.5 jit_solution(14019644171814390539)
XLA Ops:
  0.7 50.1 %shard_map.91 = (f32[2,128,1024]{2,1,0:T(8,128)}, bf16[2,128,1024]{2,1,0:T(8,128)(2,1)}, bf16[2,128,1024]{2,1,0:T(8,128)(2,1)}) custom-call(f32[1,2,128,1024]{3,2,1,0:T(8,128)} %tile_hbm.1, f32[2,256,256]{2,1,0:T(8,128)} %probe_hbm.1, f32[256,256]{1,0:T(8,128)} %phase_hbm.1, f32[4,256,256]{2,1,0:T(8,128)} %meas_hbm.1, s32[4]{0:T(128)} %rows_hbm.1, ...), custom_call_target="tpu_custom_call" | custom-call | tf_op jit(solution)/shard_map/pallas_call | solution.py:392
  50.8 2.7 %add_bitcast_fusion = f32[1,2,128,1024]{3,2,1,0:T(8,128)} fusion(bf16[2,128,1024]{2,1,0:T(8,128)(2,1)} %get-tuple-element.10, f32[2,128,1024]{2,1,0:T(8,128)} %get-tuple-element.8, bf16[2,128,1024]{2,1,0:T(8,128)(2,1)} %get-tuple-element.9), kind=kLoop, calls=%fused_computation | loop fusion | flops 1048576 | bytes 3145728 | tf_op jit(solution)/shard_map/broadcast_in_dim | solution.py:406

commit v2 on v1

--- a/solution.py
+++ b/solution.py
@@ -19,16 +19,20 @@
     angles = (index[:, None] * index[None, :] % pixels) * (2.0 * math.pi / pixels)
     scale = 1.0 / math.sqrt(pixels)
     re, im = np.cos(angles) * scale, -np.sin(angles) * scale
-    first = np.block([[re, -im], [im, re]])
-    return jnp.asarray(first, F32).astype(BF16), jnp.asarray(first.T, F32).astype(BF16)
+    blocks = []
+    for parity in range(2):
+        r, i = re[parity::2, : pixels // 2], im[parity::2, : pixels // 2]
+        blocks.append(np.block([[r, -i], [i, r]]))
+    blocks = np.stack(blocks)
+    return jnp.asarray(blocks, F32).astype(BF16), jnp.asarray(blocks.swapaxes(1, 2), F32).astype(BF16)
 
 
 def kernel(
     tile_hbm, probe_hbm, phase_hbm, meas_hbm, rows_hbm, cols_hbm, live_hbm, t1_hbm, t2_hbm,
-    own_hbm, got_low, got_high,
-    rows_s, cols_s, live_s, blk, low, tile32, tile16, probe32, phase, meas, t1, t2, par_out, par_in,
-    lower, upper, crops_b, crops_a, patch, prop, psi, xs, us, grads, came,
-    strip_low, strip_high,
+    out_hbm,
+    rows_s, cols_s, live_s, blk, low, tile32, tile16, probe32, phase, meas_in, meas_out, meas, t1, t2, par_out, par_in,
+    lower, upper, crops_b, crops_a, patch, prop, psi, adjoint, xs, us, grads, came,
+    strip_low, strip_high, got_low, got_high,
     load_sem, par_sem, tile_sem_s, tile_sem_r, meas_sem,
     bx_s, bx_r, ax_s, ax_r, gb_s, gb_r, ga_s, ga_r, strip_s, strip_r,
 ):
@@ -57,16 +61,17 @@
         pltpu.make_async_copy(rows_hbm, rows_s, load_sem.at[6]),
         pltpu.make_async_copy(cols_hbm, cols_s, load_sem.at[7]),
         pltpu.make_async_copy(live_hbm, live_s, load_sem.at[8]),
+        pltpu.make_async_copy(meas_hbm.at[depth], meas_in, load_sem.at[9]),
     ]
-    for load in loads:
-        load.start()
+    for at in (6, 7, 8, 0, 1, 9, 3, 2, 4, 5):
+        loads[at].start()
 
     barrier = pltpu.get_barrier_semaphore()
     for offset in range(1, n_depth):
         pl.semaphore_signal(barrier, inc=1, device_id=peer(offset), device_id_type=MESH)
     pl.semaphore_signal(barrier, inc=1, device_id=(depth, after), device_id_type=MESH)
     pl.semaphore_signal(barrier, inc=1, device_id=(depth, before), device_id_type=MESH)
-    for load in loads[6:]:
+    for load in loads[6:9]:
         load.wait()
     for slot in range(slots):
         par_out[slot : slot + 1, :] = jnp.full((1, width), rows_s[slot], jnp.int32)
@@ -96,9 +101,6 @@
         for copy in pair:
             copy.start()
         tile_copies.append(pair)
-    meas_copy = send(meas_hbm.at[depth], meas, meas_sem.at[0], meas_sem.at[1], (depth, after))
-    meas_copy.start()
-
     par_copy.wait_recv()
     row_at = lax.broadcasted_iota(jnp.int32, (half, width), 0)
     lane_at = lax.broadcasted_iota(jnp.int32, (rows, width), 1)
@@ -133,10 +135,29 @@
             copy.start()
             b_copies.append(copy)
 
-    loads[2].wait()
-    loads[3].wait()
     big_row = lax.broadcasted_iota(jnp.int32, (width, width), 0)
     big_lane = lax.broadcasted_iota(jnp.int32, (width, width), 1)
+    to_split = jnp.where(2 * (big_row & (half - 1)) + (big_row // half) == big_lane, 1.0, 0.0).astype(BF16)
+    of_split = jnp.where(2 * (big_lane & (half - 1)) + (big_lane // half) == big_row, 1.0, 0.0).astype(BF16)
+
+    def split_order(value, parts):
+        total = jnp.zeros_like(value)
+        for _ in range(parts):
+            part = value.astype(BF16)
+            value = value - part.astype(F32)
+            moved = jnp.dot(to_split, part, preferred_element_type=F32).astype(BF16)
+            total = total + jnp.dot(moved, of_split, preferred_element_type=F32)
+        return total
+
+    loads[9].wait()
+    meas_out[...] = split_order(meas_in[...], 3)
+    meas_copy = send(meas_out, meas, meas_sem.at[0], meas_sem.at[1], (depth, after))
+    meas_copy.start()
+    loads[3].wait()
+    phase[...] = split_order(phase[...], 3)
+    prop[0] = jnp.cos(phase[...])
+
+    loads[2].wait()
     own_row = jnp.broadcast_to(par_in[pl.ds(depth, 1), :], (width, width))
     own_col = jnp.broadcast_to(par_in[pl.ds(slots + depth, 1), :], (width, width))
     down = jnp.where(((big_row - own_row) & (width - 1)) == big_lane, 1.0, 0.0).astype(BF16)
@@ -145,8 +166,6 @@
         rolled = jnp.dot(down, probe32[plane].astype(BF16), preferred_element_type=F32)
         rolled = jnp.dot(rolled.astype(BF16), across, preferred_element_type=F32)
         psi[0, plane] = rolled.astype(BF16)
-    prop[0] = jnp.cos(phase[...])
-    prop[1] = jnp.sin(phase[...])
 
     a_copies = []
     for number, (plane, span) in enumerate(chunks):
@@ -169,19 +188,54 @@
                 copy.start()
                 a_copies.append(copy)
 
+    prop[1] = jnp.sin(phase[...])
     loads[4].wait()
     loads[5].wait()
-
-    def transform(left, right):
-        inner = jnp.dot(left[...], xs[...], preferred_element_type=F32)
-        us[:, :width] = inner[:width].astype(BF16)
-        us[:, width:] = inner[width:].astype(BF16)
-        both = jnp.dot(us[...], right[...], preferred_element_type=F32)
-        return both[:, :width], both[:, width:]
-
-    def keep(re, im):
-        xs[:width] = re.astype(BF16)
-        xs[width:] = im.astype(BF16)
+    sides = [slice(0, half), slice(half, width)]
+
+    def to_frequencies(upper_re, upper_im, lower_re, lower_im):
+        xs[0, :half] = (upper_re + lower_re).astype(BF16)
+        xs[0, half:] = (upper_im + lower_im).astype(BF16)
+        xs[1, :half] = (upper_re - lower_re).astype(BF16)
+        xs[1, half:] = (upper_im - lower_im).astype(BF16)
+        for parity in range(2):
+            inner = jnp.dot(t1[parity], xs[parity], preferred_element_type=F32)
+            for part in range(2):
+                left, right = inner[sides[part], :half], inner[sides[part], half:]
+                us[0, sides[parity], sides[part]] = (left + right).astype(BF16)
+                us[1, sides[parity], sides[part]] = (left - right).astype(BF16)
+        return [
+            jnp.dot(us[parity], t2[parity], preferred_element_type=F32) for parity in range(2)
+        ]
+
+    def keep(parity, re, im):
+        for part in range(2):
+            xs[part, :half, sides[parity]] = re[sides[part]].astype(BF16)
+            xs[part, half:, sides[parity]] = im[sides[part]].astype(BF16)
+
+    def to_positions():
+        even = jnp.dot(t2[0], xs[0], preferred_element_type=F32)
+        odd = jnp.dot(t2[1], xs[1], preferred_element_type=F32)
+        for part in range(2):
+            upper_half = (even[sides[part]] + odd[sides[part]]).astype(BF16)
+            lower_half = (even[sides[part]] - odd[sides[part]]).astype(BF16)
+            for parity in range(2):
+                us[parity, :half, sides[part]] = upper_half[:, sides[parity]]
+                us[parity, half:, sides[part]] = lower_half[:, sides[parity]]
+        even = jnp.dot(us[0], t1[0], preferred_element_type=F32)
+        odd = jnp.dot(us[1], t1[1], preferred_element_type=F32)
+        return [
+            jnp.concatenate([even[:, side] + odd[:, side], even[:, side] - odd[:, side]], axis=1)
+            for side in sides
+        ]
+
+    def propagate(halves, sign):
+        both = to_frequencies(*halves)
+        for parity in range(2):
+            re, im = both[parity][:, :half], both[parity][:, half:]
+            pr, pi = prop[0, :, sides[parity]], sign * prop[1, :, sides[parity]]
+            keep(parity, re * pr - im * pi, re * pi + im * pr)
+        return to_positions()
 
     def forward(at, carry):
         @pl.when(at != depth)
@@ -194,30 +248,31 @@
                      ax_s.at[offset, number], ax_r.at[offset, number],
                      (at, scan)).wait_recv()
 
+        halves = []
         for part in range(2):
-            span = slice(part * half, (part + 1) * half)
             tr, ti = patch[at, part, 0].astype(F32), patch[at, part, 1].astype(F32)
-            pr, pi = psi[at, 0, span].astype(F32), psi[at, 1, span].astype(F32)
-            xs[part * half : (part + 1) * half] = (tr * pr - ti * pi).astype(BF16)
-            xs[width + part * half : width + (part + 1) * half] = (tr * pi + ti * pr).astype(BF16)
-        re, im = transform(t1, t2)
-        keep(re * prop[0] - im * prop[1], re * prop[1] + im * prop[0])
-        re, im = transform(t2, t1)
+            pr, pi = psi[at, 0, sides[part]].astype(F32), psi[at, 1, sides[part]].astype(F32)
+            halves += [tr * pr - ti * pi, tr * pi + ti * pr]
+        re, im = propagate(halves, 1.0)
         psi[at + 1, 0] = re.astype(BF16)
         psi[at + 1, 1] = im.astype(BF16)
         return carry
 
     lax.fori_loop(0, n_depth, forward, 0)
 
-    xs[:width] = psi[n_depth, 0]
-    xs[width:] = psi[n_depth, 1]
-    re, im = transform(t1, t2)
+    leaving = [psi[n_depth, plane, side].astype(F32) for side in sides for plane in range(2)]
+    both = to_frequencies(*leaving)
     meas_copy.wait_recv()
-    live = jnp.where(jnp.broadcast_to(par_in[2 * slots : 2 * slots + 1, :], (width, width)) > depth, 1.0, 0.0)
-    factor = live * (1.0 - meas[...] / jnp.sqrt(re * re + im * im + 1.0))
-    keep(factor * re, factor * im)
-    re, im = transform(t2, t1)
-    keep(re, im)
+    live = jnp.where(
+        jnp.broadcast_to(par_in[2 * slots : 2 * slots + 1, :half], (width, half)) > depth, 1.0, 0.0
+    )
+    for parity in range(2):
+        re, im = both[parity][:, :half], both[parity][:, half:]
+        factor = live * (1.0 - meas[:, sides[parity]] / jnp.sqrt(re * re + im * im + 1.0))
+        keep(parity, factor * re, factor * im)
+    re, im = to_positions()
+    adjoint[0] = re
+    adjoint[1] = im
 
     def grad_near(at):
         offset = lax.rem(at + n_depth - depth, n_depth) - 1
@@ -234,18 +289,15 @@
 
     def backward(step, carry):
         at = n_depth - 1 - step
-        re, im = transform(t1, t2)
-        keep(re * prop[0] + im * prop[1], im * prop[0] - re * prop[1])
-        mu_re, mu_im = transform(t2, t1)
+        mu_re, mu_im = propagate([adjoint[plane, side] for side in sides for plane in range(2)], -1.0)
         for part in range(2):
-            span = slice(part * half, (part + 1) * half)
-            re, im = mu_re[span], mu_im[span]
+            re, im = mu_re[sides[part]], mu_im[sides[part]]
             tr, ti = patch[at, part, 0].astype(F32), patch[at, part, 1].astype(F32)
-            pr, pi = psi[at, 0, span].astype(F32), psi[at, 1, span].astype(F32)
+            pr, pi = psi[at, 0, sides[part]].astype(F32), psi[at, 1, sides[part]].astype(F32)
             grads[at, part, 0] = (pr * re + pi * im).astype(BF16)
             grads[at, part, 1] = (pr * im - pi * re).astype(BF16)
-            xs[part * half : (part + 1) * half] = (tr * re + ti * im).astype(BF16)
-            xs[width + part * half : width + (part + 1) * half] = (tr * im - ti * re).astype(BF16)
+            adjoint[0, sides[part]] = tr * re + ti * im
+            adjoint[1, sides[part]] = tr * im - ti * re
 
         @pl.when(at != depth)
         def _():
@@ -314,12 +366,17 @@
                 ]
                 total = (terms[0] + terms[1]) + (terms[2] + terms[3])
                 tile32[plane, at_rows, columns(at)] = total
-        store = pltpu.make_async_copy(tile32.at[plane], own_hbm.at[plane], load_sem.at[plane])
+    for number, (plane, span) in enumerate(chunks):
+        for copy in strip_copies[number]:
+            copy.wait_recv()
+        tile32[plane, span] = tile32[plane, span] + (
+            got_low[plane, span].astype(F32) + got_high[plane, span].astype(F32)
+        )
+        store = pltpu.make_async_copy(
+            tile32.at[plane, span], out_hbm.at[0, plane, span], load_sem.at[number]
+        )
         store.start()
         stores.append(store)
-    for pair in strip_copies:
-        for copy in pair:
-            copy.wait_recv()
     for store in stores:
         store.wait()
 
@@ -355,8 +412,10 @@
         pltpu.VMEM((2, width, width), F32),
         pltpu.VMEM((width, width), F32),
         pltpu.VMEM((width, width), F32),
-        pltpu.VMEM((2 * width, 2 * width), BF16),
-        pltpu.VMEM((2 * width, 2 * width), BF16),
+        pltpu.VMEM((width, width), F32),
+        pltpu.VMEM((width, width), F32),
+        pltpu.VMEM((2, width, width), BF16),
+        pltpu.VMEM((2, width, width), BF16),
         pltpu.VMEM((16, width), jnp.int32),
         pltpu.VMEM((16, width), jnp.int32),
         pltpu.VMEM((2, half, columns), BF16),
@@ -366,13 +425,16 @@
         pltpu.VMEM((n_depth, 2, 2, half, width), BF16),
         pltpu.VMEM((2, width, width), F32),
         pltpu.VMEM((n_depth + 1, 2, width, width), BF16),
-        pltpu.VMEM((2 * width, width), BF16),
-        pltpu.VMEM((width, 2 * width), BF16),
+        pltpu.VMEM((2, width, width), F32),
+        pltpu.VMEM((2, width, width), BF16),
+        pltpu.VMEM((2, width, width), BF16),
         pltpu.VMEM((n_depth, 2, 2, half, width), BF16),
         pltpu.VMEM((n_depth, 2, 2, half, width), BF16),
         pltpu.VMEM((2, half, columns), BF16),
         pltpu.VMEM((2, half, columns), BF16),
-        dma((9,)),
+        pltpu.VMEM((2, half, columns), BF16),
+        pltpu.VMEM((2, half, columns), BF16),
+        dma((10,)),
         dma((2,)),
         dma((2, 4)),
         dma((2, 4)),
@@ -389,21 +451,16 @@
         dma((2, 4)),
     ]
     anywhere = pl.BlockSpec(memory_space=pltpu.HBM)
-    own, from_after, from_before = pl.pallas_call(
+    return pl.pallas_call(
         kernel,
-        out_shape=[
-            jax.ShapeDtypeStruct((2, half, columns), F32),
-            jax.ShapeDtypeStruct((2, half, columns), BF16),
-            jax.ShapeDtypeStruct((2, half, columns), BF16),
-        ],
+        out_shape=jax.ShapeDtypeStruct(transmission.shape, F32),
         in_specs=[anywhere] * 9,
-        out_specs=[anywhere] * 3,
+        out_specs=anywhere,
         scratch_shapes=scratch,
         compiler_params=pltpu.CompilerParams(
             collective_id=0, has_side_effects=True, vmem_limit_bytes=67_000_000
         ),
     )(transmission, probe_wave, prop_phase, measured, scan_rows, scan_cols, live_counts, t1, t2)
-    return (own + from_after.astype(F32) + from_before.astype(F32))[None]
 
 
 def solution(mesh):

time: 53.6 us -> 49.7 us (0.927)
  Pallas kernels: 50.1 us -> 46.6 us
  other arithmetic: 2.73 us -> 0 us
  local copies, waits for them, and re-layouts: 0 us -> 2.31 us
    pallas_call x1, Pallas kernels: 50.1 us -> 46.6 us  [body(): pl.pallas_call(kernel, out_shape=jax.ShapeDtypeStruct(transmission.shape,...]
    broadcast_in_dim x1 -> x0, other arithmetic: 2.73 us -> none  [body(): return (own + from_after.astype(F32) + from_before.astype(F32))[None]]
    unnamed x0 -> x1, local copies, waits for them, and re-layouts: none -> 2.31 us
where the time goes in v2:
time: 49.7 us; the launch traced here: 49.5 us
  Pallas kernels  46.6 us (94%)
  local copies, waits for them, and re-layouts  2.31 us (5%)
  between operations  0.66 us (1%)
    pallas_call x1, Pallas kernels, body(): pl.pallas_call(kernel, out_shape=jax.ShapeDtypeStruct(transmission.shape,...  46.6 us
    unnamed x1, local copies, waits for them, and re-layouts  2.31 us

profile of v2, /device:TPU:0, one launch (start us, length us, event | category | flops | bytes accessed | tf_op | source)
XLA Modules:
  0.0 49.5 jit_solution(841094289986521823)
XLA Ops:
  0.7 46.6 %shard_map.91 = f32[1,2,128,1024]{3,2,1,0:T(8,128)} custom-call(f32[1,2,128,1024]{3,2,1,0:T(8,128)} %tile_hbm.1, f32[2,256,256]{2,1,0:T(8,128)} %probe_hbm.1, f32[256,256]{1,0:T(8,128)} %phase_hbm.1, f32[4,256,256]{2,1,0:T(8,128)} %meas_hbm.1, s32[4]{0:T(128)} %rows_hbm.1, s32[4]{0:T(128)} %cols_hbm.1, s32[1]{0:T(128)S(6)} %copy.11.live_hbm, ...), custom_call_target="tpu_custom_call" | custom-call | tf_op jit(solution)/shard_map/pallas_call | solution.py:454
  47.2 2.3 %copy.12 = f32[1,2,128,1024]{3,2,1,0:T(8,128)} copy(f32[1,2,128,1024]{3,2,1,0:T(8,128)} %shard_map.91) | data formatting | bytes 2097152

commit v3 on v2

--- a/solution.py
+++ b/solution.py
@@ -29,7 +29,7 @@
 
 def kernel(
     tile_hbm, probe_hbm, phase_hbm, meas_hbm, rows_hbm, cols_hbm, live_hbm, t1_hbm, t2_hbm,
-    out_hbm,
+    out_ref,
     rows_s, cols_s, live_s, blk, low, tile32, tile16, probe32, phase, meas_in, meas_out, meas, t1, t2, par_out, par_in,
     lower, upper, crops_b, crops_a, patch, prop, psi, adjoint, xs, us, grads, came,
     strip_low, strip_high, got_low, got_high,
@@ -121,7 +121,7 @@
         return slice(at * width, (at + 1) * width)
 
     b_copies = []
-    for offset in range(n_depth):
+    for offset in (*range(1, n_depth), 0):
         slot = lax.rem(depth + offset, n_depth)
         for plane, span in chunks:
             piece = pick(slot, [tile16[plane, span, columns(at)] for at in range(blocks)])
@@ -171,7 +171,7 @@
     for number, (plane, span) in enumerate(chunks):
         for copy in tile_copies[number]:
             copy.wait_recv()
-        for offset in (1, 3, 2, 0) if n_depth == 4 else range(n_depth):
+        for offset in (*range(1, n_depth), 0):
             slot = lax.rem(depth + offset, n_depth)
             is_low = low[slot, span] > 0.5
             piece = pick(slot, [
@@ -308,8 +308,12 @@
 
     lax.fori_loop(0, n_depth, backward, 0)
 
-    for back in range(n_depth):
-        at = n_depth - 1 - back
+    @pl.when(depth != 0)
+    def _():
+        for copy in grad_near(0):
+            copy.wait_send()
+
+    for at in range(n_depth):
 
         @pl.when(at != depth)
         def _(at=at):
@@ -354,7 +358,6 @@
     for offset in range(n_depth - 1):
         send(grads.at[0, 1], came.at[0, 1], gb_s.at[offset], gb_r.at[offset],
              (depth, scan)).wait_recv()
-    stores = []
     for plane in range(2):
         for piece in range(4):
             at_rows = slice(piece * (rows // 2), (piece + 1) * (rows // 2))
@@ -365,20 +368,13 @@
                     for slot in range(slots)
                 ]
                 total = (terms[0] + terms[1]) + (terms[2] + terms[3])
-                tile32[plane, at_rows, columns(at)] = total
+                out_ref[0, plane, at_rows, columns(at)] = total
     for number, (plane, span) in enumerate(chunks):
         for copy in strip_copies[number]:
             copy.wait_recv()
-        tile32[plane, span] = tile32[plane, span] + (
+        out_ref[0, plane, span] = out_ref[0, plane, span] + (
             got_low[plane, span].astype(F32) + got_high[plane, span].astype(F32)
         )
-        store = pltpu.make_async_copy(
-            tile32.at[plane, span], out_hbm.at[0, plane, span], load_sem.at[number]
-        )
-        store.start()
-        stores.append(store)
-    for store in stores:
-        store.wait()
 
     par_copy.wait_send()
     meas_copy.wait_send()
@@ -389,8 +385,12 @@
             copy.wait_send()
     for step in range(1, n_depth):
         at = lax.rem(depth + step, n_depth)
-        for copy in grad_near(at) + [grad_far(at)]:
-            copy.wait_send()
+        grad_far(at).wait_send()
+
+        @pl.when(at != 0)
+        def _(at=at):
+            for copy in grad_near(at):
+                copy.wait_send()
 
 
 def body(transmission, probe_wave, prop_phase, measured, scan_rows, scan_cols, live_counts):
@@ -453,12 +453,12 @@
     anywhere = pl.BlockSpec(memory_space=pltpu.HBM)
     return pl.pallas_call(
         kernel,
-        out_shape=jax.ShapeDtypeStruct(transmission.shape, F32),
+        out_shape=pltpu.VMEM(transmission.shape, F32),
         in_specs=[anywhere] * 9,
-        out_specs=anywhere,
+        out_specs=pl.BlockSpec(memory_space=pltpu.VMEM),
         scratch_shapes=scratch,
         compiler_params=pltpu.CompilerParams(
-            collective_id=0, has_side_effects=True, vmem_limit_bytes=67_000_000
+            collective_id=0, has_side_effects=True, vmem_limit_bytes=57_000_000
         ),
     )(transmission, probe_wave, prop_phase, measured, scan_rows, scan_cols, live_counts, t1, t2)
 

time: 49.7 us -> 51.6 us (1.038)
  the two profiles are of different devices: /device:TPU:0 before, /device:TPU:6 now
where the time goes in v3:
time: 51.6 us; the launch traced here: 51.5 us
  Pallas kernels  49.9 us (97%)
  local copies, waits for them, and re-layouts  0.97 us (2%)
  between operations  0.66 us (1%)
    pallas_call x1, Pallas kernels, body(): pl.pallas_call(kernel, out_shape=pltpu.VMEM(transmission.shape, F32), in_...  49.9 us

profile of v3, /device:TPU:6, one launch (start us, length us, event | category | flops | bytes accessed | tf_op | source)
XLA Modules:
  0.0 51.5 jit_solution(7794130650450460226)
XLA Ops:
  0.7 49.9 %shard_map.91 = f32[1,2,128,1024]{3,2,1,0:T(8,128)S(1)} custom-call(f32[1,2,128,1024]{3,2,1,0:T(8,128)} %tile_hbm.1, f32[2,256,256]{2,1,0:T(8,128)} %probe_hbm.1, f32[256,256]{1,0:T(8,128)} %phase_hbm.1, f32[4,256,256]{2,1,0:T(8,128)} %meas_hbm.1, s32[4]{0:T(128)} %rows_hbm.1, s32[4]{0:T(128)} %cols_hbm.1, s32[1]{0:T(128)S(6)} %copy.12.live_hbm, ...), custom_call_target="tpu_custom_call" | custom-call | tf_op jit(solution)/shard_map/pallas_call | solution.py:454
  50.6 1.0 %copy.11 = f32[1,2,128,1024]{3,2,1,0:T(8,128)} copy(f32[1,2,128,1024]{3,2,1,0:T(8,128)S(1)} %shard_map.91) | data formatting | bytes 2097152

commit v4 on v3

--- a/solution.py
+++ b/solution.py
@@ -308,12 +308,8 @@
 
     lax.fori_loop(0, n_depth, backward, 0)
 
-    @pl.when(depth != 0)
-    def _():
-        for copy in grad_near(0):
-            copy.wait_send()
-
-    for at in range(n_depth):
+    for back in range(n_depth):
+        at = n_depth - 1 - back
 
         @pl.when(at != depth)
         def _(at=at):
@@ -385,12 +381,8 @@
             copy.wait_send()
     for step in range(1, n_depth):
         at = lax.rem(depth + step, n_depth)
-        grad_far(at).wait_send()
-
-        @pl.when(at != 0)
-        def _(at=at):
-            for copy in grad_near(at):
-                copy.wait_send()
+        for copy in grad_near(at) + [grad_far(at)]:
+            copy.wait_send()
 
 
 def body(transmission, probe_wave, prop_phase, measured, scan_rows, scan_cols, live_counts):

time: 51.6 us -> 47.6 us (0.922)
  the two profiles are of different devices: /device:TPU:6 before, /device:TPU:0 now
where the time goes in v4:
time: 47.6 us; the launch traced here: 47.5 us
  Pallas kernels  45.8 us (96%)
  local copies, waits for them, and re-layouts  0.97 us (2%)
  between operations  0.66 us (1%)
    pallas_call x1, Pallas kernels, body(): pl.pallas_call(kernel, out_shape=pltpu.VMEM(transmission.shape, F32), in_...  45.8 us
    unnamed x1, local copies, waits for them, and re-layouts  0.97 us

profile of v4, /device:TPU:0, one launch (start us, length us, event | category | flops | bytes accessed | tf_op | source)
XLA Modules:
  0.0 47.5 jit_solution(11494870594349570304)
XLA Ops:
  0.7 45.8 %shard_map.91 = f32[1,2,128,1024]{3,2,1,0:T(8,128)S(1)} custom-call(f32[1,2,128,1024]{3,2,1,0:T(8,128)} %tile_hbm.1, f32[2,256,256]{2,1,0:T(8,128)} %probe_hbm.1, f32[256,256]{1,0:T(8,128)} %phase_hbm.1, f32[4,256,256]{2,1,0:T(8,128)} %meas_hbm.1, s32[4]{0:T(128)} %rows_hbm.1, s32[4]{0:T(128)} %cols_hbm.1, s32[1]{0:T(128)S(6)} %copy.12.live_hbm, ...), custom_call_target="tpu_custom_call" | custom-call | tf_op jit(solution)/shard_map/pallas_call | solution.py:446
  46.5 1.0 %copy.11 = f32[1,2,128,1024]{3,2,1,0:T(8,128)} copy(f32[1,2,128,1024]{3,2,1,0:T(8,128)S(1)} %shard_map.91) | data formatting | bytes 2097152

commit v5 on v4

--- a/solution.py
+++ b/solution.py
@@ -46,11 +46,17 @@
     blocks = tile32.shape[2] // width
     slots = n_depth
     rows = half // 2
+    order = (n_depth // 2, *(at for at in range(1, n_depth) if at != n_depth // 2), 0)
     chunks = [(plane, slice(part * rows, (part + 1) * rows)) for plane in range(2) for part in range(2)]
 
     def peer(offset):
         return (lax.rem(depth + offset, n_depth), scan)
 
+    barrier = pltpu.get_barrier_semaphore()
+    for offset in range(1, n_depth):
+        pl.semaphore_signal(barrier, inc=1, device_id=peer(offset), device_id_type=MESH)
+    pl.semaphore_signal(barrier, inc=1, device_id=(depth, after), device_id_type=MESH)
+    pl.semaphore_signal(barrier, inc=1, device_id=(depth, before), device_id_type=MESH)
     loads = [
         pltpu.make_async_copy(tile_hbm.at[0, 0], tile32.at[0], load_sem.at[0]),
         pltpu.make_async_copy(tile_hbm.at[0, 1], tile32.at[1], load_sem.at[1]),
@@ -66,11 +72,6 @@
     for at in (6, 7, 8, 0, 1, 9, 3, 2, 4, 5):
         loads[at].start()
 
-    barrier = pltpu.get_barrier_semaphore()
-    for offset in range(1, n_depth):
-        pl.semaphore_signal(barrier, inc=1, device_id=peer(offset), device_id_type=MESH)
-    pl.semaphore_signal(barrier, inc=1, device_id=(depth, after), device_id_type=MESH)
-    pl.semaphore_signal(barrier, inc=1, device_id=(depth, before), device_id_type=MESH)
     for load in loads[6:9]:
         load.wait()
     for slot in range(slots):
@@ -108,8 +109,6 @@
         first = jnp.broadcast_to(par_in[slots + slot : slots + slot + 1, :], (rows, width))
         block = (first >> 8) + jnp.where(lane_at < (first & (width - 1)), 1, 0)
         blk[slot] = block.astype(F32).astype(BF16)
-        begin = jnp.broadcast_to(par_in[slot : slot + 1, :], (half, width))
-        low[slot] = jnp.where(row_at >= begin, 1.0, 0.0).astype(BF16)
 
     def pick(slot, values):
         piece = values[0]
@@ -121,7 +120,7 @@
         return slice(at * width, (at + 1) * width)
 
     b_copies = []
-    for offset in (*range(1, n_depth), 0):
+    for offset in order:
         slot = lax.rem(depth + offset, n_depth)
         for plane, span in chunks:
             piece = pick(slot, [tile16[plane, span, columns(at)] for at in range(blocks)])
@@ -135,6 +134,10 @@
             copy.start()
             b_copies.append(copy)
 
+    for slot in range(slots):
+        begin = jnp.broadcast_to(par_in[slot : slot + 1, :], (half, width))
+        low[slot] = jnp.where(row_at >= begin, 1.0, 0.0).astype(BF16)
+
     big_row = lax.broadcasted_iota(jnp.int32, (width, width), 0)
     big_lane = lax.broadcasted_iota(jnp.int32, (width, width), 1)
     to_split = jnp.where(2 * (big_row & (half - 1)) + (big_row // half) == big_lane, 1.0, 0.0).astype(BF16)
@@ -171,7 +174,7 @@
     for number, (plane, span) in enumerate(chunks):
         for copy in tile_copies[number]:
             copy.wait_recv()
-        for offset in (*range(1, n_depth), 0):
+        for offset in order:
             slot = lax.rem(depth + offset, n_depth)
             is_low = low[slot, span] > 0.5
             piece = pick(slot, [
@@ -298,11 +301,12 @@
             grads[at, part, 1] = (pr * im - pi * re).astype(BF16)
             adjoint[0, sides[part]] = tr * re + ti * im
             adjoint[1, sides[part]] = tr * im - ti * re
-
-        @pl.when(at != depth)
-        def _():
-            for copy in grad_near(at):
-                copy.start()
+            if part == 0:
+
+                @pl.when(at != depth)
+                def _():
+                    for copy in grad_near(at):
+                        copy.start()
 
         return carry
 

time: 47.6 us -> 47 us (0.987)
  Pallas kernels: 45.8 us -> 45.3 us
    pallas_call x1, Pallas kernels: 45.8 us -> 45.3 us  [body(): pl.pallas_call(kernel, out_shape=pltpu.VMEM(transmission.shape, F32), in_...]
where the time goes in v5:
time: 47 us; the launch traced here: 46.9 us
  Pallas kernels  45.3 us (96%)
  local copies, waits for them, and re-layouts  0.97 us (2%)
  between operations  0.66 us (1%)
    pallas_call x1, Pallas kernels, body(): pl.pallas_call(kernel, out_shape=pltpu.VMEM(transmission.shape, F32), in_...  45.3 us
    unnamed x1, local copies, waits for them, and re-layouts  0.97 us

profile of v5, /device:TPU:0, one launch (start us, length us, event | category | flops | bytes accessed | tf_op | source)
XLA Modules:
  0.0 46.9 jit_solution(4543847829004528911)
XLA Ops:
  0.7 45.3 %shard_map.91 = f32[1,2,128,1024]{3,2,1,0:T(8,128)S(1)} custom-call(f32[1,2,128,1024]{3,2,1,0:T(8,128)} %tile_hbm.1, f32[2,256,256]{2,1,0:T(8,128)} %probe_hbm.1, f32[256,256]{1,0:T(8,128)} %phase_hbm.1, f32[4,256,256]{2,1,0:T(8,128)} %meas_hbm.1, s32[4]{0:T(128)} %rows_hbm.1, s32[4]{0:T(128)} %cols_hbm.1, s32[1]{0:T(128)S(6)} %copy.12.live_hbm, ...), custom_call_target="tpu_custom_call" | custom-call | tf_op jit(solution)/shard_map/pallas_call | solution.py:450
  45.9 1.0 %copy.11 = f32[1,2,128,1024]{3,2,1,0:T(8,128)} copy(f32[1,2,128,1024]{3,2,1,0:T(8,128)S(1)} %shard_map.91) | data formatting | bytes 2097152

commit v6 on v5

--- a/solution.py
+++ b/solution.py
@@ -271,7 +271,7 @@
     )
     for parity in range(2):
         re, im = both[parity][:, :half], both[parity][:, half:]
-        factor = live * (1.0 - meas[:, sides[parity]] / jnp.sqrt(re * re + im * im + 1.0))
+        factor = live * (1.0 - meas[:, sides[parity]] * lax.rsqrt(re * re + im * im + 1.0))
         keep(parity, factor * re, factor * im)
     re, im = to_positions()
     adjoint[0] = re

time: 47 us -> 46.9 us (level)
  no operation moved by 1% of the time
where the time goes in v6:
time: 46.9 us; the launch traced here: 46.8 us
  Pallas kernels  45.2 us (96%)
  local copies, waits for them, and re-layouts  0.97 us (2%)
  between operations  0.66 us (1%)
    pallas_call x1, Pallas kernels, body(): pl.pallas_call(kernel, out_shape=pltpu.VMEM(transmission.shape, F32), in_...  45.2 us
    unnamed x1, local copies, waits for them, and re-layouts  0.97 us

profile of v6, /device:TPU:0, one launch (start us, length us, event | category | flops | bytes accessed | tf_op | source)
XLA Modules:
  0.0 46.8 jit_solution(1240384785095743660)
XLA Ops:
  0.7 45.2 %shard_map.91 = f32[1,2,128,1024]{3,2,1,0:T(8,128)S(1)} custom-call(f32[1,2,128,1024]{3,2,1,0:T(8,128)} %tile_hbm.1, f32[2,256,256]{2,1,0:T(8,128)} %probe_hbm.1, f32[256,256]{1,0:T(8,128)} %phase_hbm.1, f32[4,256,256]{2,1,0:T(8,128)} %meas_hbm.1, s32[4]{0:T(128)} %rows_hbm.1, s32[4]{0:T(128)} %cols_hbm.1, s32[1]{0:T(128)S(6)} %copy.12.live_hbm, ...), custom_call_target="tpu_custom_call" | custom-call | tf_op jit(solution)/shard_map/pallas_call | solution.py:450
  45.8 1.0 %copy.11 = f32[1,2,128,1024]{3,2,1,0:T(8,128)} copy(f32[1,2,128,1024]{3,2,1,0:T(8,128)S(1)} %shard_map.91) | data formatting | bytes 2097152

commit v7 on v6

--- a/solution.py
+++ b/solution.py
@@ -328,30 +328,28 @@
         for offset in range(n_depth - 1):
             send(grads.at[0, 0, plane, span], came.at[0, 0, plane, span], ga_s.at[offset, number],
                  ga_r.at[offset, number], (depth, scan)).wait_recv()
-        for piece in range(2):
-            start = span.start + piece * (rows // 2)
-            at_rows = slice(start, start + rows // 2)
-            lows, highs = [], []
-            for slot in range(slots):
-                value = came[slot, 0, plane, at_rows]
-                is_low = low[slot, at_rows] > 0.5
-                lows.append(jnp.where(is_low, value, zero))
-                highs.append(jnp.where(is_low, zero, value))
-            for at in range(blocks):
-                for target, values in ((strip_low, lows), (strip_high, highs)):
-                    terms = [
-                        jnp.where(blk[slot, : rows // 2] == at, values[slot], zero)
-                        for slot in range(slots)
-                    ]
-                    total = (terms[0] + terms[1]) + (terms[2] + terms[3])
-                    target[plane, at_rows, columns(at)] = total
         pair = [
             send(strip_low.at[plane, span], got_low.at[plane, span], strip_s.at[0, number],
                  strip_r.at[0, number], (depth, before)),
             send(strip_high.at[plane, span], got_high.at[plane, span], strip_s.at[1, number],
                  strip_r.at[1, number], (depth, after)),
         ]
-        for copy in pair:
+        for target, copy, is_high in ((strip_high, pair[1], True), (strip_low, pair[0], False)):
+            for start in range(span.start, span.stop, rows // 2):
+                at_rows = slice(start, start + rows // 2)
+                values = []
+                for slot in range(slots):
+                    value = came[slot, 0, plane, at_rows]
+                    is_low = low[slot, at_rows] > 0.5
+                    values.append(
+                        jnp.where(is_low, zero, value) if is_high else jnp.where(is_low, value, zero)
+                    )
+                for at in range(blocks):
+                    terms = [
+                        jnp.where(blk[slot, : rows // 2] == at, values[slot], zero)
+                        for slot in range(slots)
+                    ]
+                    target[plane, at_rows, columns(at)] = (terms[0] + terms[1]) + (terms[2] + terms[3])
             copy.start()
         strip_copies.append(pair)
 

time: 46.9 us -> 46.9 us (level)
  no operation moved by 1% of the time
where the time goes in v7:
time: 46.9 us; the launch traced here: 46.8 us
  Pallas kernels  45.1 us (96%)
  local copies, waits for them, and re-layouts  0.97 us (2%)
  between operations  0.66 us (1%)
    pallas_call x1, Pallas kernels, body(): pl.pallas_call(kernel, out_shape=pltpu.VMEM(transmission.shape, F32), in_...  45.1 us
    unnamed x1, local copies, waits for them, and re-layouts  0.97 us

profile of v7, /device:TPU:0, one launch (start us, length us, event | category | flops | bytes accessed | tf_op | source)
XLA Modules:
  0.0 46.8 jit_solution(17094414478888027926)
XLA Ops:
  0.7 45.1 %shard_map.91 = f32[1,2,128,1024]{3,2,1,0:T(8,128)S(1)} custom-call(f32[1,2,128,1024]{3,2,1,0:T(8,128)} %tile_hbm.1, f32[2,256,256]{2,1,0:T(8,128)} %probe_hbm.1, f32[256,256]{1,0:T(8,128)} %phase_hbm.1, f32[4,256,256]{2,1,0:T(8,128)} %meas_hbm.1, s32[4]{0:T(128)} %rows_hbm.1, s32[4]{0:T(128)} %cols_hbm.1, s32[1]{0:T(128)S(6)} %copy.12.live_hbm, ...), custom_call_target="tpu_custom_call" | custom-call | tf_op jit(solution)/shard_map/pallas_call | solution.py:448
  45.8 1.0 %copy.11 = f32[1,2,128,1024]{3,2,1,0:T(8,128)} copy(f32[1,2,128,1024]{3,2,1,0:T(8,128)S(1)} %shard_map.91) | data formatting | bytes 2097152
